TPU v7x, 128 devices: a whole 4x4x4 slice. The times are simulated.
128 devices in a mesh: req: 32 (over x, z, core), tp: 4 (over y).
Axes of the slice: x: 4, y: 4, z: 4, core: 2. Of those that a mesh axis runs over, the one named last changes fastest.
Arguments:
- hidden_states: bfloat16 [8192, 2048], P('req'), may hold values from -30 to 30
- norm_gain: float32 [2048], replicated, may hold values from 0.5 to 1.5
- head: bfloat16 [2048, 98304], P(None, ('req', 'tp')), may hold values from -1 to 1
- target_ids: int32 [8192], P('req'), may hold values from 0 to 98303
- lengths: int32 [32], P('req'), may hold values from 32 to 256, as said below
Outputs:
- token_logprob: float32 [8192], P('req')
- token_entropy: float32 [8192], P('req')
- seq_mean_logprob: float32 [32], P('req')
- seq_top_logit: float32 [32], P('req')
Inputs may be any that keep to these rules, and one draw needn't show every extreme that they name: `lengths`: each completion has at least 32 and at most 256 live slots; some completion has exactly 256.
All inputs are finite; a program needn't handle non-finite values.
Results may differ from a plain program's by a relative error of at most 0.0018.
Values may be sent and summed in bfloat16 or wider, within the bound.
A program may use at most 128 MiB of HBM per device.

v0:
```python
import math
import jax
import jax.numpy as jnp
from jax import lax
from jax.sharding import PartitionSpec as P


def combined_all(value, axis, combine):
    everything = jax.tree.map(lambda part: lax.all_gather(part, axis), value)
    leading = jax.tree.map(lambda part: part[0], everything)

    def turn(k, so_far):
        return combine(so_far, jax.tree.map(lambda part: part[k], everything))

    return lax.fori_loop(1, lax.axis_size(axis), turn, leading)


def combine(first, second):
    top = jnp.maximum(first[0], second[0])
    left = jnp.exp(first[0] - top)
    right = jnp.exp(second[0] - top)
    return (
        top,
        first[1] * left + second[1] * right,
        first[2] * left + second[2] * right,
        first[3] + second[3],
    )


def block_stats(block, target, matrix, vocab_ids):
    logits = jnp.dot(block, matrix, preferred_element_type=jnp.float32)
    top = jnp.max(logits, axis=-1)
    shifted = jnp.exp(logits - top[:, None])
    weight_sum = jnp.sum(shifted, axis=-1)
    weighted = jnp.sum(shifted * logits, axis=-1)
    hit = vocab_ids == target[:, None]
    picked = jnp.sum(jnp.where(hit, logits, 0.0), axis=-1)
    return (top, weight_sum, weighted, picked)


def blocked_stats(block, target, matrix, vocab_ids):
    count = block.shape[0]
    step = math.gcd(count, 512)
    stats = lax.map(
        lambda a: block_stats(a[0], a[1], matrix, vocab_ids),
        (block.reshape(count // step, step, block.shape[1]), target.reshape(count // step, step)),
    )
    return tuple((s.reshape(-1) for s in stats))


def per_device(hidden_states, norm_gain, head, target_ids, lengths):
    feats = hidden_states.astype(jnp.float32)
    scale = lax.rsqrt(jnp.mean(feats * feats, axis=-1, keepdims=True) + 1e-06)
    normed = (feats * scale * norm_gain).astype(jnp.bfloat16)
    rows = hidden_states.shape[0]
    vdev = head.shape[1]
    n_req = lax.axis_size("req")
    n_tp = lax.axis_size("tp")
    my_req = lax.axis_index("req")
    vbase = (my_req * n_tp + lax.axis_index("tp")) * vdev
    columns = lax.broadcasted_iota(jnp.int32, (1, vdev), 1)
    own_vocab = columns + vbase
    block = lax.all_gather(normed, "req", axis=0, tiled=True)
    target = lax.all_gather(target_ids, "req", axis=0, tiled=True)
    stats = blocked_stats(block, target, head, own_vocab)
    gathered = tuple((new for new in stats))
    shaped = tuple((s.reshape(n_req, rows) for s in gathered))
    arrived = (
        lax.all_to_all(shaped[0], "req", split_axis=0, concat_axis=0, tiled=True),
        lax.all_to_all(shaped[1], "req", split_axis=0, concat_axis=0, tiled=True),
        lax.all_to_all(shaped[2], "req", split_axis=0, concat_axis=0, tiled=True),
        lax.all_to_all(shaped[3], "req", split_axis=0, concat_axis=0, tiled=True),
    )
    top = jnp.max(arrived[0], axis=0)
    factor = jnp.exp(arrived[0] - top[None, :])
    own = (
        top,
        jnp.sum(arrived[1] * factor, axis=0),
        jnp.sum(arrived[2] * factor, axis=0),
        jnp.sum(arrived[3], axis=0),
    )
    merged = combined_all((own[0], own[1], own[2], own[3]), "tp", combine)
    top, weight_sum, weighted, picked = merged
    log_norm = top + jnp.log(weight_sum)
    live = jnp.arange(rows, dtype=jnp.int32) < lengths[0]
    logprob = jnp.where(live, picked - log_norm, jnp.float32(0.0))
    entropy = jnp.where(live, log_norm - weighted / weight_sum, jnp.float32(0.0))
    mean_lp = (jnp.sum(logprob) / lengths[0].astype(jnp.float32)).reshape(1)
    top_live = jnp.max(jnp.where(live, top, jnp.float32(-1e30))).reshape(1)
    return (logprob, entropy, mean_lp, top_live)


def solution(mesh):
    in_specs = (P("req", None), P(), P(None, ("req", "tp")), P("req"), P("req"))
    out_specs = (P("req"), P("req"), P("req"), P("req"))
    return jax.shard_map(
        per_device, mesh=mesh, in_specs=in_specs, out_specs=out_specs, check_vma=False
    )
```

profile of v0, /device:TPU:14, one launch (start us, length us, event | category | flops | bytes accessed | tf_op | source)
XLA Modules:
  0.0 283.6 jit_solution(8951670508299853403)
XLA Ops:
  7.2 1.7 fusion.7
  8.9 2.5 fusion.9
  11.5 25.2 %all-gather.4 = s32[32,1,256]{2,1,0:T(1,128)S(1)} all-gather(s32[1,1,256]{2,1,0:T(1,128)S(1)} %bitcast.102), channel_id=1, replica_groups=mesh['req'=32,'tp'=4] {'req'}, dimensions={0}, use_global_device_ids=true | all-gather | bytes 33792 | tf_op jit(solution)/shard_map/all_gather | solution.py:64
  36.7 0.1 reduce.3
  36.8 91.0 %all-gather.11.cloned.1.call-done = bf16[8192,2048]{1,0:T(8,128)(2,1)} async-done(((bf16[256,2048]{1,0:T(8,128)(2,1)}), bf16[8192,2048]{1,0:T(8,128)(2,1)}) %all-gather.11.cloned.1.call-update) | async-done | bytes 33554448 | tf_op jit(solution)/shard_map/all_gather | solution.py:63
  127.8 72.3 %while.39 = (s32[]{:T(128)}, f32[16,512]{1,0:T(8,128)S(1)}, f32[16,512]{1,0:T(8,128)S(1)}, f32[16,512]{1,0:T(8,128)S(1)}, f32[16,512]{1,0:T(8,128)S(1)}, /*index...) while((s32[]{:T(128)}, f32[16,512]{1,0:T(8,128)S(1)}, ...), condition=%wide.region_6.7_spmd.clone, body=%wide.region_1.6_spmd.clone.sunk | while | flops 1613757184 | bytes 8428165 | solution.py:44
  127.8 3.5 %fusion.19 = (f32[512]{0:T(512)S(1)}, f32[512,768]{1,0:T(8,128)S(1)}) fusion(bf16[2048,768]{1,0:T(8,128)(2,1)S(1)} %get-tuple-element.519, bf16[16,512,2048]{2,1,0:T(8,128)(2,1)} %get-tuple-element.518, s32[]{:T(128)} %get-tuple-element.502), kind=kOutput, calls=%fused_computation.41.clone.1 | convolution fusion | flops 1611005440 | bytes 6818304 | tf_op jit(solution)/shard_map/while/body/eval_jaxpr/dot_general | solution.py:31
  131.3 0.7 multiply_reduce_fusion.2
  132.2 0.1 dynamic_update_slice.22
  132.2 0.1 dynamic_update_slice.21
  132.3 3.5 %fusion.19 = (f32[512]{0:T(512)S(1)}, f32[512,768]{1,0:T(8,128)S(1)}) fusion(bf16[2048,768]{1,0:T(8,128)(2,1)S(1)} %get-tuple-element.519, bf16[16,512,2048]{2,1,0:T(8,128)(2,1)} %get-tuple-element.518, s32[]{:T(128)} %get-tuple-element.502), kind=kOutput, calls=%fused_computation.41.clone.1 | convolution fusion | flops 1611005440 | bytes 6818304 | tf_op jit(solution)/shard_map/while/body/eval_jaxpr/dot_general | solution.py:31
  135.8 0.7 multiply_reduce_fusion.2
  136.7 0.1 dynamic_update_slice.22
  136.8 0.1 dynamic_update_slice.21
  136.8 3.5 %fusion.19 = (f32[512]{0:T(512)S(1)}, f32[512,768]{1,0:T(8,128)S(1)}) fusion(bf16[2048,768]{1,0:T(8,128)(2,1)S(1)} %get-tuple-element.519, bf16[16,512,2048]{2,1,0:T(8,128)(2,1)} %get-tuple-element.518, s32[]{:T(128)} %get-tuple-element.502), kind=kOutput, calls=%fused_computation.41.clone.1 | convolution fusion | flops 1611005440 | bytes 6818304 | tf_op jit(solution)/shard_map/while/body/eval_jaxpr/dot_general | solution.py:31
  140.4 0.7 multiply_reduce_fusion.2
  141.3 0.1 dynamic_update_slice.21
  141.4 3.5 %fusion.19 = (f32[512]{0:T(512)S(1)}, f32[512,768]{1,0:T(8,128)S(1)}) fusion(bf16[2048,768]{1,0:T(8,128)(2,1)S(1)} %get-tuple-element.519, bf16[16,512,2048]{2,1,0:T(8,128)(2,1)} %get-tuple-element.518, s32[]{:T(128)} %get-tuple-element.502), kind=kOutput, calls=%fused_computation.41.clone.1 | convolution fusion | flops 1611005440 | bytes 6818304 | tf_op jit(solution)/shard_map/while/body/eval_jaxpr/dot_general | solution.py:31
  144.9 0.7 multiply_reduce_fusion.2
  145.8 0.1 dynamic_update_slice.21
  145.9 3.5 %fusion.19 = (f32[512]{0:T(512)S(1)}, f32[512,768]{1,0:T(8,128)S(1)}) fusion(bf16[2048,768]{1,0:T(8,128)(2,1)S(1)} %get-tuple-element.519, bf16[16,512,2048]{2,1,0:T(8,128)(2,1)} %get-tuple-element.518, s32[]{:T(128)} %get-tuple-element.502), kind=kOutput, calls=%fused_computation.41.clone.1 | convolution fusion | flops 1611005440 | bytes 6818304 | tf_op jit(solution)/shard_map/while/body/eval_jaxpr/dot_general | solution.py:31
  149.4 0.7 multiply_reduce_fusion.2
  150.2 0.1 dynamic_update_slice.24
  150.3 0.1 dynamic_update_slice.21
  150.4 3.5 %fusion.19 = (f32[512]{0:T(512)S(1)}, f32[512,768]{1,0:T(8,128)S(1)}) fusion(bf16[2048,768]{1,0:T(8,128)(2,1)S(1)} %get-tuple-element.519, bf16[16,512,2048]{2,1,0:T(8,128)(2,1)} %get-tuple-element.518, s32[]{:T(128)} %get-tuple-element.502), kind=kOutput, calls=%fused_computation.41.clone.1 | convolution fusion | flops 1611005440 | bytes 6818304 | tf_op jit(solution)/shard_map/while/body/eval_jaxpr/dot_general | solution.py:31
  153.9 0.7 multiply_reduce_fusion.2
  154.7 0.1 dynamic_update_slice.24
  154.9 3.5 %fusion.19 = (f32[512]{0:T(512)S(1)}, f32[512,768]{1,0:T(8,128)S(1)}) fusion(bf16[2048,768]{1,0:T(8,128)(2,1)S(1)} %get-tuple-element.519, bf16[16,512,2048]{2,1,0:T(8,128)(2,1)} %get-tuple-element.518, s32[]{:T(128)} %get-tuple-element.502), kind=kOutput, calls=%fused_computation.41.clone.1 | convolution fusion | flops 1611005440 | bytes 6818304 | tf_op jit(solution)/shard_map/while/body/eval_jaxpr/dot_general | solution.py:31
  158.4 0.7 multiply_reduce_fusion.2
  159.4 3.5 %fusion.19 = (f32[512]{0:T(512)S(1)}, f32[512,768]{1,0:T(8,128)S(1)}) fusion(bf16[2048,768]{1,0:T(8,128)(2,1)S(1)} %get-tuple-element.519, bf16[16,512,2048]{2,1,0:T(8,128)(2,1)} %get-tuple-element.518, s32[]{:T(128)} %get-tuple-element.502), kind=kOutput, calls=%fused_computation.41.clone.1 | convolution fusion | flops 1611005440 | bytes 6818304 | tf_op jit(solution)/shard_map/while/body/eval_jaxpr/dot_general | solution.py:31
  162.9 0.7 multiply_reduce_fusion.2
  164.0 3.5 %fusion.19 = (f32[512]{0:T(512)S(1)}, f32[512,768]{1,0:T(8,128)S(1)}) fusion(bf16[2048,768]{1,0:T(8,128)(2,1)S(1)} %get-tuple-element.519, bf16[16,512,2048]{2,1,0:T(8,128)(2,1)} %get-tuple-element.518, s32[]{:T(128)} %get-tuple-element.502), kind=kOutput, calls=%fused_computation.41.clone.1 | convolution fusion | flops 1611005440 | bytes 6818304 | tf_op jit(solution)/shard_map/while/body/eval_jaxpr/dot_general | solution.py:31
  167.5 0.7 multiply_reduce_fusion.2
  168.5 3.5 %fusion.19 = (f32[512]{0:T(512)S(1)}, f32[512,768]{1,0:T(8,128)S(1)}) fusion(bf16[2048,768]{1,0:T(8,128)(2,1)S(1)} %get-tuple-element.519, bf16[16,512,2048]{2,1,0:T(8,128)(2,1)} %get-tuple-element.518, s32[]{:T(128)} %get-tuple-element.502), kind=kOutput, calls=%fused_computation.41.clone.1 | convolution fusion | flops 1611005440 | bytes 6818304 | tf_op jit(solution)/shard_map/while/body/eval_jaxpr/dot_general | solution.py:31
  172.0 0.7 multiply_reduce_fusion.2
  173.0 3.5 %fusion.19 = (f32[512]{0:T(512)S(1)}, f32[512,768]{1,0:T(8,128)S(1)}) fusion(bf16[2048,768]{1,0:T(8,128)(2,1)S(1)} %get-tuple-element.519, bf16[16,512,2048]{2,1,0:T(8,128)(2,1)} %get-tuple-element.518, s32[]{:T(128)} %get-tuple-element.502), kind=kOutput, calls=%fused_computation.41.clone.1 | convolution fusion | flops 1611005440 | bytes 6818304 | tf_op jit(solution)/shard_map/while/body/eval_jaxpr/dot_general | solution.py:31
  176.5 0.7 multiply_reduce_fusion.2
  177.5 3.5 %fusion.19 = (f32[512]{0:T(512)S(1)}, f32[512,768]{1,0:T(8,128)S(1)}) fusion(bf16[2048,768]{1,0:T(8,128)(2,1)S(1)} %get-tuple-element.519, bf16[16,512,2048]{2,1,0:T(8,128)(2,1)} %get-tuple-element.518, s32[]{:T(128)} %get-tuple-element.502), kind=kOutput, calls=%fused_computation.41.clone.1 | convolution fusion | flops 1611005440 | bytes 6818304 | tf_op jit(solution)/shard_map/while/body/eval_jaxpr/dot_general | solution.py:31
  181.0 0.7 multiply_reduce_fusion.2
  182.0 3.5 %fusion.19 = (f32[512]{0:T(512)S(1)}, f32[512,768]{1,0:T(8,128)S(1)}) fusion(bf16[2048,768]{1,0:T(8,128)(2,1)S(1)} %get-tuple-element.519, bf16[16,512,2048]{2,1,0:T(8,128)(2,1)} %get-tuple-element.518, s32[]{:T(128)} %get-tuple-element.502), kind=kOutput, calls=%fused_computation.41.clone.1 | convolution fusion | flops 1611005440 | bytes 6818304 | tf_op jit(solution)/shard_map/while/body/eval_jaxpr/dot_general | solution.py:31
  185.5 0.7 multiply_reduce_fusion.2
  186.6 3.5 %fusion.19 = (f32[512]{0:T(512)S(1)}, f32[512,768]{1,0:T(8,128)S(1)}) fusion(bf16[2048,768]{1,0:T(8,128)(2,1)S(1)} %get-tuple-element.519, bf16[16,512,2048]{2,1,0:T(8,128)(2,1)} %get-tuple-element.518, s32[]{:T(128)} %get-tuple-element.502), kind=kOutput, calls=%fused_computation.41.clone.1 | convolution fusion | flops 1611005440 | bytes 6818304 | tf_op jit(solution)/shard_map/while/body/eval_jaxpr/dot_general | solution.py:31
  190.1 0.7 multiply_reduce_fusion.2
  191.1 3.5 %fusion.19 = (f32[512]{0:T(512)S(1)}, f32[512,768]{1,0:T(8,128)S(1)}) fusion(bf16[2048,768]{1,0:T(8,128)(2,1)S(1)} %get-tuple-element.519, bf16[16,512,2048]{2,1,0:T(8,128)(2,1)} %get-tuple-element.518, s32[]{:T(128)} %get-tuple-element.502), kind=kOutput, calls=%fused_computation.41.clone.1 | convolution fusion | flops 1611005440 | bytes 6818304 | tf_op jit(solution)/shard_map/while/body/eval_jaxpr/dot_general | solution.py:31
  194.6 0.7 multiply_reduce_fusion.2
  195.6 3.5 %fusion.19 = (f32[512]{0:T(512)S(1)}, f32[512,768]{1,0:T(8,128)S(1)}) fusion(bf16[2048,768]{1,0:T(8,128)(2,1)S(1)} %get-tuple-element.519, bf16[16,512,2048]{2,1,0:T(8,128)(2,1)} %get-tuple-element.518, s32[]{:T(128)} %get-tuple-element.502), kind=kOutput, calls=%fused_computation.41.clone.1 | convolution fusion | flops 1611005440 | bytes 6818304 | tf_op jit(solution)/shard_map/while/body/eval_jaxpr/dot_general | solution.py:31
  199.1 0.7 multiply_reduce_fusion.2
  200.1 0.6 all_to_all.30
  200.8 5.6 %all-to-all-start = ((f32[32,1,256]{2,1,0:T(1,128)}), f32[32,1,256]{2,1,0:T(1,128)S(1)}, u32[]{:S(2)}, u32[]{:S(2)}) async-start(f32[32,1,256]{2,1,0:T(1,128)} %all_to_all.30), calls=%async_computation | async-start | bytes 65536 | tf_op jit(solution)/shard_map/all_to_all | solution.py:69
  206.3 0.6 all_to_all.32
  207.0 4.9 %all-to-all-done = f32[32,1,256]{2,1,0:T(1,128)S(1)} async-done(((f32[32,1,256]{2,1,0:T(1,128)}), f32[32,1,256]{2,1,0:T(1,128)S(1)}, u32[]{:S(2)}, u32[]{:S(2)}) %all-to-all-start) | async-done | bytes 32800 | tf_op jit(solution)/shard_map/all_to_all | solution.py:69
  211.9 5.7 %all-to-all-start.1 = ((f32[32,1,256]{2,1,0:T(1,128)}), f32[32,1,256]{2,1,0:T(1,128)S(1)}, u32[]{:S(2)}, u32[]{:S(2)}) async-start(f32[32,1,256]{2,1,0:T(1,128)} %all_to_all.32), calls=%async_computation.1 | async-start | bytes 65536 | tf_op jit(solution)/shard_map/all_to_all | solution.py:70
  217.6 0.6 all_to_all.36
  218.2 4.8 %all-to-all-done.1 = f32[32,1,256]{2,1,0:T(1,128)S(1)} async-done(((f32[32,1,256]{2,1,0:T(1,128)}), f32[32,1,256]{2,1,0:T(1,128)S(1)}, u32[]{:S(2)}, u32[]{:S(2)}) %all-to-all-start.1) | async-done | bytes 32800 | tf_op jit(solution)/shard_map/all_to_all | solution.py:70
  223.1 5.8 %all-to-all-start.2 = ((f32[32,1,256]{2,1,0:T(1,128)}), f32[32,1,256]{2,1,0:T(1,128)S(1)}, u32[]{:S(2)}, u32[]{:S(2)}) async-start(f32[32,1,256]{2,1,0:T(1,128)} %all_to_all.36), calls=%async_computation.2 | async-start | bytes 65536 | tf_op jit(solution)/shard_map/all_to_all | solution.py:71
  229.5 0.6 all_to_all.39
  230.2 4.1 %all-to-all-done.2 = f32[32,1,256]{2,1,0:T(1,128)S(1)} async-done(((f32[32,1,256]{2,1,0:T(1,128)}), f32[32,1,256]{2,1,0:T(1,128)S(1)}, u32[]{:S(2)}, u32[]{:S(2)}) %all-to-all-start.2) | async-done | bytes 32800 | tf_op jit(solution)/shard_map/all_to_all | solution.py:71
  234.4 5.8 %all-to-all-start.3 = ((f32[32,1,256]{2,1,0:T(1,128)}), f32[32,1,256]{2,1,0:T(1,128)S(1)}, u32[]{:S(2)}, u32[]{:S(2)}) async-start(f32[32,1,256]{2,1,0:T(1,128)} %all_to_all.39), calls=%async_computation.3 | async-start | bytes 65536 | tf_op jit(solution)/shard_map/all_to_all | solution.py:72
  240.2 7.8 %all-gather.6 = f32[4,1,256]{2,1,0:T(1,128)S(1)} all-gather(f32[1,1,256]{2,1,0:T(1,128)S(1)} %bitcast.100), channel_id=3, replica_groups=mesh['req'=32,'tp'=4] {'tp'}, dimensions={0}, use_global_device_ids=true | all-gather | bytes 5120 | tf_op jit(solution)/shard_map/all_gather | solution.py:9
  248.0 9.4 %all-gather.7 = f32[4,1,256]{2,1,0:T(1,128)S(1)} all-gather(f32[1,1,256]{2,1,0:T(1,128)S(1)} %bitcast.99), channel_id=4, replica_groups=mesh['req'=32,'tp'=4] {'tp'}, dimensions={0}, use_global_device_ids=true | all-gather | bytes 5120 | tf_op jit(solution)/shard_map/all_gather | solution.py:9
  257.4 7.0 %all-gather.5 = f32[4,1,256]{2,1,0:T(1,128)S(1)} all-gather(f32[1,1,256]{2,1,0:T(1,128)S(1)} %bitcast.98), channel_id=2, replica_groups=mesh['req'=32,'tp'=4] {'tp'}, dimensions={0}, use_global_device_ids=true | all-gather | bytes 5120 | tf_op jit(solution)/shard_map/all_gather | solution.py:9
  264.4 9.0 %all-gather.8 = f32[4,1,256]{2,1,0:T(1,128)S(1)} all-gather(f32[1,1,256]{2,1,0:T(1,128)S(1)} %bitcast.101), channel_id=5, replica_groups=mesh['req'=32,'tp'=4] {'tp'}, dimensions={0}, use_global_device_ids=true | all-gather | bytes 5120 | tf_op jit(solution)/shard_map/all_gather | solution.py:9
  273.4 0.3 while.38
  273.7 1.2 fusion.13
  (129 shorter events, 4.3 us)
Async XLA Ops:
  7.2 4.3 %copy-start = (s32[256]{0:T(256)S(1)}, s32[256]{0:T(256)}, u32[]{:S(2)}) copy-start(s32[256]{0:T(256)} %param.12) | copy-start | bytes 3076
  7.2 120.6 %copy-start.1 = (bf16[2048,768]{1,0:T(8,128)(2,1)S(1)}, bf16[2048,768]{1,0:T(8,128)(2,1)}, u32[]{:S(2)}) copy-start(bf16[2048,768]{1,0:T(8,128)(2,1)} %param.11) | copy-start | bytes 9437188
  7.2 120.6 %all-gather.11.cloned.1.call-start = ((), (), s32[]{:S(2)}) async-start(), calls=%async_computation.4 | async-start | bytes 34603008 | tf_op jit(solution)/shard_map/all_gather | solution.py:63
  200.8 11.1 %all-to-all-start = ((f32[32,1,256]{2,1,0:T(1,128)}), f32[32,1,256]{2,1,0:T(1,128)S(1)}, u32[]{:S(2)}, u32[]{:S(2)}) async-start(f32[32,1,256]{2,1,0:T(1,128)} %all_to_all.30), calls=%async_computation | async-start | bytes 65536 | tf_op jit(solution)/shard_map/all_to_all | solution.py:69
  211.9 11.2 %all-to-all-start.1 = ((f32[32,1,256]{2,1,0:T(1,128)}), f32[32,1,256]{2,1,0:T(1,128)S(1)}, u32[]{:S(2)}, u32[]{:S(2)}) async-start(f32[32,1,256]{2,1,0:T(1,128)} %all_to_all.32), calls=%async_computation.1 | async-start | bytes 65536 | tf_op jit(solution)/shard_map/all_to_all | solution.py:70
  223.1 11.3 %all-to-all-start.2 = ((f32[32,1,256]{2,1,0:T(1,128)}), f32[32,1,256]{2,1,0:T(1,128)S(1)}, u32[]{:S(2)}, u32[]{:S(2)}) async-start(f32[32,1,256]{2,1,0:T(1,128)} %all_to_all.36), calls=%async_computation.2 | async-start | bytes 65536 | tf_op jit(solution)/shard_map/all_to_all | solution.py:71
  234.4 30.0 %all-to-all-start.3 = ((f32[32,1,256]{2,1,0:T(1,128)}), f32[32,1,256]{2,1,0:T(1,128)S(1)}, u32[]{:S(2)}, u32[]{:S(2)}) async-start(f32[32,1,256]{2,1,0:T(1,128)} %all_to_all.39), calls=%async_computation.3 | async-start | bytes 65536 | tf_op jit(solution)/shard_map/all_to_all | solution.py:72
Sparse Core Ops, SparseCore 0:
  11.6 116.1 all-gather.10
where the time goes:
time: 284 us
  waiting for transfers between devices  105 us (37%)
  blocking collectives  58.3 us (21%)
  matrix products  55.4 us (20%)
  starting transfers between devices  22.9 us (8%)
  other arithmetic  17.6 us (6%)
  between operations  16.6 us (6%)
  local copies, waits for them, and re-layouts  6.78 us (2%)
    all_gather x1, waiting for transfers between devices, per_device(): block = lax.all_gather(normed, 'req', axis=0, tiled=True)  91 us
    dot_general x16, matrix products, block_stats(): logits = jnp.dot(block, matrix, preferred_element_type=jnp.float32)  55.4 us
    all_gather x4, blocking collectives, combined_all(): everything = jax.tree.map(lambda part: lax.all_gather(part, axis), value)  33.2 us
    all_gather x1, blocking collectives, per_device(): target = lax.all_gather(target_ids, 'req', axis=0, tiled=True)  25.2 us
    reduce_sum x16, other arithmetic, block_stats(): weighted = jnp.sum(shifted * logits, axis=-1)  11.5 us
    all_to_all x1, starting transfers between devices, per_device(): lax.all_to_all(shaped[2], 'req', split_axis=0, concat_axis=0, tiled=True)  5.79 us
    all_to_all x1, starting transfers between devices, per_device(): lax.all_to_all(shaped[3], 'req', split_axis=0, concat_axis=0, tiled=True)  5.77 us
    all_to_all x1, starting transfers between devices, per_device(): lax.all_to_all(shaped[1], 'req', split_axis=0, concat_axis=0, tiled=True)  5.72 us
  transfers between devices with their start and end apart: 5, of which 4 were waited for; matrix products, arithmetic and copies ran while one was open for 0% of the time, Pallas kernels for 0%

commit v1 on v0

--- a/solution.py
+++ b/solution.py
@@ -60,7 +60,10 @@
     vbase = (my_req * n_tp + lax.axis_index("tp")) * vdev
     columns = lax.broadcasted_iota(jnp.int32, (1, vdev), 1)
     own_vocab = columns + vbase
-    block = lax.all_gather(normed, "req", axis=0, tiled=True)
+    reach_marks = lambda base_x, mesh_ax, dim_no: jnp.concatenate(
+        jax.lax.all_to_all(jnp.stack(jax.lax.axis_size(mesh_ax) * [base_x]), mesh_ax, 0, 0), dim_no
+    )
+    block = reach_marks(normed, "req", 0)
     target = lax.all_gather(target_ids, "req", axis=0, tiled=True)
     stats = blocked_stats(block, target, head, own_vocab)
     gathered = tuple((new for new in stats))

time: 284 us -> 735 us (2.59)
  blocking collectives: 58.3 us -> 595 us
  waiting for transfers between devices: 105 us -> 13.9 us
  between operations: 16.6 us -> 3.22 us
  local copies, waits for them, and re-layouts: 6.78 us -> 17.8 us
  starting transfers between devices: 22.9 us -> 31.7 us
    all_gather x1, blocking collectives: 25.2 us -> 562 us  [per_device(): target = lax.all_gather(target_ids, 'req', axis=0, tiled=True)]
    all_gather x1 -> x0, waiting for transfers between devices: 91 us -> none  [per_device(): block = lax.all_gather(normed, 'req', axis=0, tiled=True)]
    another operation x0 -> x1, local copies, waits for them, and re-layouts: none -> 11 us  [per_device(): jnp.stack(jax.lax.axis_size(mesh_ax) * [base_x])]
    all_to_all x0 -> x1, starting transfers between devices: none -> 8.77 us  [per_device(): jax.lax.all_to_all(jnp.stack(jax.lax.axis_size(mesh_ax) * [base_x]), mesh...]
  transfers between devices with their start and end apart: 5 -> 5, of which waited for: 4 -> 3; matrix products, arithmetic and copies ran while one was open for 0% -> 0% of each run, Pallas kernels for 0% -> 0%
where the time goes in v1:
time: 735 us; the launch traced here: 734 us
  blocking collectives  595 us (81%)
  matrix products  55.4 us (8%)
  starting transfers between devices  31.7 us (4%)
  local copies, waits for them, and re-layouts  17.8 us (2%)
  other arithmetic  16.4 us (2%)
  waiting for transfers between devices  13.9 us (2%)
    all_gather x1, blocking collectives, per_device(): target = lax.all_gather(target_ids, 'req', axis=0, tiled=True)  562 us
    dot_general x16, matrix products, block_stats(): logits = jnp.dot(block, matrix, preferred_element_type=jnp.float32)  55.4 us
    all_gather x4, blocking collectives, combined_all(): everything = jax.tree.map(lambda part: lax.all_gather(part, axis), value)  33.3 us
  transfers between devices with their start and end apart: 5, of which 3 were waited for; matrix products, arithmetic and copies ran while one was open for 0% of the time, Pallas kernels for 0%

profile of v1, /device:TPU:14, one launch (start us, length us, event | category | flops | bytes accessed | tf_op | source)
XLA Modules:
  0.0 734.4 jit_solution(10193787667716911730)
XLA Ops:
  0.6 1.5 fusion.7
  2.2 1.5 fusion.9
  3.7 11.0 %stack.2 = bf16[32,256,2048]{2,1,0:T(8,128)(2,1)} broadcast(bf16[256,2048]{1,0:T(8,128)(2,1)S(1)} %fusion.9), dimensions={1,2} | broadcast | bytes 34603008 | tf_op jit(solution)/shard_map/stack | solution.py:64
  14.7 8.8 %all-to-all-start = ((bf16[32,256,2048]{2,1,0:T(8,128)(2,1)}), bf16[32,256,2048]{2,1,0:T(8,128)(2,1)}, u32[]{:S(2)}, u32[]{:S(2)}) async-start(bf16[32,256,2048]{2,1,0:T(8,128)(2,1)} %stack.2), calls=%async_computation | async-start | bytes 67108864 | tf_op jit(solution)/shard_map/all_to_all | solution.py:64
  23.6 561.7 %all-gather.4 = s32[32,1,256]{2,1,0:T(1,128)S(1)} all-gather(s32[1,1,256]{2,1,0:T(1,128)S(1)} %bitcast.102), channel_id=1, replica_groups=mesh['req'=32,'tp'=4] {'req'}, dimensions={0}, use_global_device_ids=true | all-gather | bytes 33792 | tf_op jit(solution)/shard_map/all_gather | solution.py:67
  585.2 0.1 reduce.3
  585.3 72.2 %while.39 = (s32[]{:T(128)}, f32[16,512]{1,0:T(8,128)S(1)}, f32[16,512]{1,0:T(8,128)S(1)}, f32[16,512]{1,0:T(8,128)S(1)}, f32[16,512]{1,0:T(8,128)S(1)}, /*index...) while((s32[]{:T(128)}, f32[16,512]{1,0:T(8,128)S(1)}, ...), condition=%wide.region_6.7_spmd.clone, body=%wide.region_1.6_spmd.clone.sunk | while | flops 1613757184 | bytes 8428165 | solution.py:44
  585.3 3.5 fusion.19
  588.9 0.7 multiply_reduce_fusion.2
  589.8 0.1 dynamic_update_slice.21
  589.9 3.5 fusion.19
  593.4 0.7 multiply_reduce_fusion.2
  594.2 0.1 dynamic_update_slice.22
  594.3 0.1 dynamic_update_slice.21
  594.4 3.5 fusion.19
  597.9 0.7 multiply_reduce_fusion.2
  598.7 0.1 dynamic_update_slice.24
  598.7 0.1 dynamic_update_slice.22
  598.9 3.5 fusion.19
  602.4 0.7 multiply_reduce_fusion.2
  603.2 0.1 dynamic_update_slice.24
  603.3 0.1 dynamic_update_slice.22
  603.4 3.5 fusion.19
  606.9 0.7 multiply_reduce_fusion.2
  607.7 0.1 dynamic_update_slice.24
  607.9 3.5 fusion.19
  611.4 0.7 multiply_reduce_fusion.2
  612.4 3.5 fusion.19
  615.9 0.7 multiply_reduce_fusion.2
  617.0 3.5 fusion.19
  620.5 0.7 multiply_reduce_fusion.2
  621.5 3.5 fusion.19
  625.0 0.7 multiply_reduce_fusion.2
  626.0 3.5 fusion.19
  629.5 0.7 multiply_reduce_fusion.2
  630.5 3.5 fusion.19
  634.0 0.7 multiply_reduce_fusion.2
  635.0 3.5 fusion.19
  638.5 0.7 multiply_reduce_fusion.2
  639.5 3.5 fusion.19
  643.0 0.7 multiply_reduce_fusion.2
  644.0 3.5 fusion.19
  647.5 0.7 multiply_reduce_fusion.2
  648.5 3.5 fusion.19
  652.0 0.7 multiply_reduce_fusion.2
  653.1 3.5 fusion.19
  656.6 0.7 multiply_reduce_fusion.2
  657.6 0.6 all_to_all.34
  658.2 5.6 all-to-all-start.1
  663.8 0.6 all_to_all.36
  664.5 4.9 all-to-all-done.1
  669.4 5.7 all-to-all-start.2
  675.1 0.6 all_to_all.40
  675.7 4.8 all-to-all-done.2
  680.6 5.8 all-to-all-start.3
  687.0 0.6 all_to_all.43
  687.7 4.1 all-to-all-done.3
  691.9 5.8 all-to-all-start.4
  697.7 7.9 %all-gather.6 = f32[4,1,256]{2,1,0:T(1,128)S(1)} all-gather(f32[1,1,256]{2,1,0:T(1,128)S(1)} %bitcast.100), channel_id=3, replica_groups=mesh['req'=32,'tp'=4] {'tp'}, dimensions={0}, use_global_device_ids=true | all-gather | bytes 5120 | tf_op jit(solution)/shard_map/all_gather | solution.py:9
  705.6 9.4 %all-gather.7 = f32[4,1,256]{2,1,0:T(1,128)S(1)} all-gather(f32[1,1,256]{2,1,0:T(1,128)S(1)} %bitcast.99), channel_id=4, replica_groups=mesh['req'=32,'tp'=4] {'tp'}, dimensions={0}, use_global_device_ids=true | all-gather | bytes 5120 | tf_op jit(solution)/shard_map/all_gather | solution.py:9
  715.1 7.0 all-gather.5
  722.1 9.0 %all-gather.8 = f32[4,1,256]{2,1,0:T(1,128)S(1)} all-gather(f32[1,1,256]{2,1,0:T(1,128)S(1)} %bitcast.101), channel_id=5, replica_groups=mesh['req'=32,'tp'=4] {'tp'}, dimensions={0}, use_global_device_ids=true | all-gather | bytes 5120 | tf_op jit(solution)/shard_map/all_gather | solution.py:9
  731.1 0.3 while.38
  731.4 1.2 fusion.13
  (129 shorter events, 4.3 us)
Async XLA Ops:
  14.7 8.8 %copy-start = (s32[256]{0:T(256)S(1)}, s32[256]{0:T(256)}, u32[]{:S(2)}) copy-start(s32[256]{0:T(256)} %param.12) | copy-start | bytes 3076
  14.7 570.6 %copy-start.1 = (bf16[2048,768]{1,0:T(8,128)(2,1)S(1)}, bf16[2048,768]{1,0:T(8,128)(2,1)}, u32[]{:S(2)}) copy-start(bf16[2048,768]{1,0:T(8,128)(2,1)} %param.11) | copy-start | bytes 9437188
  14.7 570.6 %all-to-all-start = ((bf16[32,256,2048]{2,1,0:T(8,128)(2,1)}), bf16[32,256,2048]{2,1,0:T(8,128)(2,1)}, u32[]{:S(2)}, u32[]{:S(2)}) async-start(bf16[32,256,2048]{2,1,0:T(8,128)(2,1)} %stack.2), calls=%async_computation | async-start | bytes 67108864 | tf_op jit(solution)/shard_map/all_to_all | solution.py:64
  658.2 11.1 %all-to-all-start.1 = ((f32[32,1,256]{2,1,0:T(1,128)}), f32[32,1,256]{2,1,0:T(1,128)S(1)}, u32[]{:S(2)}, u32[]{:S(2)}) async-start(f32[32,1,256]{2,1,0:T(1,128)} %all_to_all.34), calls=%async_computation.1 | async-start | bytes 65536 | tf_op jit(solution)/shard_map/all_to_all | solution.py:72
  669.4 11.2 %all-to-all-start.2 = ((f32[32,1,256]{2,1,0:T(1,128)}), f32[32,1,256]{2,1,0:T(1,128)S(1)}, u32[]{:S(2)}, u32[]{:S(2)}) async-start(f32[32,1,256]{2,1,0:T(1,128)} %all_to_all.36), calls=%async_computation.2 | async-start | bytes 65536 | tf_op jit(solution)/shard_map/all_to_all | solution.py:73
  680.6 11.3 %all-to-all-start.3 = ((f32[32,1,256]{2,1,0:T(1,128)}), f32[32,1,256]{2,1,0:T(1,128)S(1)}, u32[]{:S(2)}, u32[]{:S(2)}) async-start(f32[32,1,256]{2,1,0:T(1,128)} %all_to_all.40), calls=%async_computation.3 | async-start | bytes 65536 | tf_op jit(solution)/shard_map/all_to_all | solution.py:74
  691.9 30.2 %all-to-all-start.4 = ((f32[32,1,256]{2,1,0:T(1,128)}), f32[32,1,256]{2,1,0:T(1,128)S(1)}, u32[]{:S(2)}, u32[]{:S(2)}) async-start(f32[32,1,256]{2,1,0:T(1,128)} %all_to_all.43), calls=%async_computation.4 | async-start | bytes 65536 | tf_op jit(solution)/shard_map/all_to_all | solution.py:75
